TPU v7x, 32 devices: a whole 2x2x4 slice. The times are simulated.
32 devices in a mesh: groups: 2 (over x), ctx: 16 (over z, y, core).
Axes of the slice: x: 2, y: 2, z: 4, core: 2. Of those that a mesh axis runs over, the one named last changes fastest.
Arguments:
- hidden: bfloat16 [256, 8192], P('groups', 'ctx'), parts along dimension 0, may hold values from -6 to 6
- attn_gain: bfloat16 [8192], P('ctx'), may hold values from 0.25 to 1.75
- q_weight: bfloat16 [8192, 8192], P(None, 'ctx'), may hold values from -0.0625 to 0.0625
- q_gain: bfloat16 [128], replicated, may hold values from 0.25 to 1.75
- key_cache: bfloat16 [49152, 1024], P(('groups', 'ctx')), parts along dimension 0, may hold values from -64 to 64
- value_cache: bfloat16 [49152, 1024], P(('groups', 'ctx')), parts along dimension 0, may hold values from -6 to 6
- block_limit: int32 [256], P('groups'), parts along dimension 0, may hold values from 0 to 191, as said below
- out_weight: bfloat16 [8192, 8192], P('ctx'), may hold values from -0.09375 to 0.09375
- next_gain: bfloat16 [8192], P('ctx'), may hold values from 0.25 to 1.75
- next_weight: bfloat16 [8192, 8192], P(None, 'ctx'), may hold values from -0.0625 to 0.0625
Outputs:
- new_hidden: bfloat16 [256, 8192], P('groups', 'ctx'), parts along dimension 0
- next_queries: bfloat16 [256, 8192], P('groups', 'ctx'), parts along dimension 0
There are 2 independent parts, one for each index of `groups`. A program takes and returns all parts, laid end to end along the dimension named above; an argument that names none is the same for every part. Nothing has to cross between parts.
Inputs may be any that keep to these rules, and one draw needn't show every extreme that they name: Text token i may attend the visual blocks 0 to block_limit[i], each of 128 visual tokens; some token reaches the last block and some only the first.
All inputs are finite; a program needn't handle non-finite values.
Results may differ from a plain program's by a relative error of at most 0.015.
Values may be sent and summed in bfloat16 or wider, within the bound.
A program may use at most 64 MiB of HBM per device.

v0:
```python
import functools
import math

import jax
import jax.numpy as jnp
from jax import lax
from jax.experimental import pallas as pl
from jax.experimental.pallas import tpu as pltpu
from jax.sharding import PartitionSpec as P

BLK = 128
EPSILON = 1e-05
MESH = pl.DeviceIdType.MESH
BF16, F32 = jnp.bfloat16, jnp.float32


def loop(count, body):
    def step(i, carry):
        body(i)
        return carry

    lax.fori_loop(0, count, step, 0)


def kernel(
    n,
    group_size,
    hidden_in,
    attn_gain_ref,
    next_gain_ref,
    q_gain_ref,
    limit_ref,
    qw_hbm,
    key_hbm,
    value_hbm,
    ow_hbm,
    nw_hbm,
    hidden_out,
    next_out,
    qw,
    keys,
    values,
    ow,
    nw,
    first,
    queries_all,
    second,
    sums,
    stats,
    mixed,
    sums_core,
    stats_core,
    mixed_core,
    sums_y,
    stats_y,
    mixed_y,
    sums_up,
    stats_up,
    mixed_up,
    sums_down,
    stats_down,
    mixed_down,
    acc,
    squares,
    limits,
    attended,
    sems,
    local_sems,
):
    depth = n // 4
    me = lax.axis_index("ctx")
    core, y, z = lax.rem(me, 2), lax.rem(me // 2, 2), me // 4
    rows, width = hidden_out.shape
    features = n * width
    head_dim = q_gain_ref.shape[1]
    heads = width // head_dim
    tokens = keys.shape[0]

    def at(zz, yy, cc):
        return zz * 4 + yy * 2 + cc

    other_core, other_y = at(z, y, 1 - core), at(z, 1 - y, core)
    above, below = at(z + 1, y, core), at(z - 1, y, core)

    loads = [
        pltpu.make_async_copy(src, dst, local_sems.at[i])
        for i, (src, dst) in enumerate(
            [
                (hidden_in, first.at[me, pl.ds(0, rows)]),
                (qw_hbm, qw),
                (key_hbm, keys),
                (value_hbm, values),
                (ow_hbm, ow),
                (nw_hbm, nw),
            ]
        )
    ]
    for load in loads:
        load.start()

    line = lax.broadcasted_iota(jnp.int32, (16, width), 0)
    gains = [jnp.broadcast_to(g[...].astype(F32), (16, width)) for g in (attn_gain_ref, next_gain_ref)]
    first[me, rows : rows + 16, :] = jnp.where(line == 0, gains[0], gains[1]).astype(BF16)

    barrier = pltpu.get_barrier_semaphore()

    def greet(device):
        pl.semaphore_signal(barrier, inc=1, device_id={"ctx": device}, device_id_type=MESH)

    greet(other_core)
    greet(other_y)
    pl.when(z + 1 < depth)(lambda: greet(above))
    pl.when(z > 0)(lambda: greet(below))
    peers = 2 + jnp.where(z + 1 < depth, 1, 0) + jnp.where(z > 0, 1, 0)
    pl.semaphore_wait(barrier, peers)

    limit_rows = jnp.broadcast_to(limit_ref[...], (rows, rows)).T[:, :1]
    for head in range(heads):
        limits[head * rows : (head + 1) * rows, :] = jnp.broadcast_to(limit_rows, (rows, BLK))

    before, after = z, depth - 1 - z
    lone, paired = jnp.abs(after - before), jnp.minimum(after, before)

    def farthest(i):
        j = jnp.maximum(i - lone, 0)
        distance = paired - lax.div(j, 2)
        near = z + jnp.where(lax.rem(j, 2) == 0, distance, -distance)
        return jnp.where(i < lone, jnp.where(after > before, depth - 1 - i, i), near)

    def remote(src, dst, send, recv, device):
        return pltpu.make_async_remote_copy(
            src_ref=src,
            dst_ref=dst,
            send_sem=sems.at[send],
            recv_sem=sems.at[recv],
            device_id={"ctx": device},
            device_id_type=MESH,
        )

    used = [0]
    drains = []

    def gather(buffer, ready, consume):
        base = used[0]
        used[0] += n + 5 * depth
        send = base + n

        def copy(block, device, sem):
            return remote(buffer.at[block], buffer.at[block], sem, base + block, device)

        def to_above(zz):
            return copy(at(zz, y, core), above, send + zz)

        def to_below(zz):
            return copy(at(zz, y, core), below, send + depth + zz)

        def to_y(zz):
            return copy(at(zz, y, core), other_y, send + 2 * depth + zz)

        def to_core(zz, yy):
            return copy(at(zz, yy, core), other_core, send + 3 * depth + 2 * zz + yy)

        def arrive(block):
            copy(block, other_core, send).wait_recv()

        def column(step, sign):
            zz = z + sign * step
            start = step == 0
            fresh = jnp.logical_not(start) if sign > 0 else step >= 0

            @pl.when((zz >= 0) & (zz < depth) & fresh)
            def _():
                pl.when(step > 0)(lambda: arrive(at(zz, y, core)))
                if sign < 0:
                    pl.when(z + 1 < depth)(lambda: to_above(zz).start())
                    pl.when(start & (z > 0))(lambda: to_below(zz).start())
                else:
                    pl.when(z > 0)(lambda: to_below(zz).start())
                to_y(zz).start()
                to_core(zz, y).start()

        def beside(step, sign):
            zz = z + sign * step

            @pl.when((zz >= 0) & (zz < depth) & (step >= (1 if sign > 0 else 0)))
            def _():
                arrive(at(zz, 1 - y, core))
                to_core(zz, 1 - y).start()

        def turn(step):
            column(step, -1)
            column(step, 1)
            beside(step - 1, -1)
            beside(step - 1, 1)
            pl.when(step == 1)(ready)

            def use(i):
                distance = step - 1
                upward = i >= 2
                zz = z + jnp.where(upward, distance, -distance)
                fresh = (distance > 0) | jnp.logical_not(upward)

                @pl.when((distance >= 0) & (zz >= 0) & (zz < depth) & fresh)
                def _():
                    consume(at(zz, lax.rem(i, 2), core))

            loop(4, use)

        loop(depth + 1, turn)

        def drain():
            def one(zz):
                pl.when((zz <= z) & (z + 1 < depth))(lambda: to_above(zz).wait_send())
                pl.when((zz >= z) & (z > 0))(lambda: to_below(zz).wait_send())
                to_y(zz).wait_send()
                to_core(zz, 0).wait_send()
                to_core(zz, 1).wait_send()

            loop(depth, one)

        drains.append(drain)
        return arrive

    def reduce(arrays, compute_other, compute, combine):
        starts = []
        for _ in arrays:
            starts.append(used[0])
            used[0] += 10 * depth

        def copies(kind, zz, yy=0):
            made = []
            for base, (part, from_core, from_y, from_below, from_above) in zip(starts, arrays):
                if kind == 0:
                    slot, room, where = 2 * zz + yy, 2 * depth, 0
                    src, dst, device = part.at[at(zz, yy, 1 - core)], from_core, other_core
                elif kind == 1:
                    slot, room, where = zz, depth, 4 * depth
                    src, dst, device = part.at[at(zz, 1 - y, core)], from_y, other_y
                elif kind == 2:
                    slot, room, where = zz, depth, 6 * depth
                    src, dst, device = part.at[at(zz, y, core)], from_below, above
                else:
                    slot, room, where = zz, depth, 8 * depth
                    src, dst, device = part.at[at(zz, y, core)], from_above, below
                sem = base + where + slot
                made.append(remote(src, dst.at[slot], sem, sem + room, device))
            return made

        def begin(*which):
            for copy in copies(*which):
                copy.start()

        def received(*which):
            for copy in copies(*which):
                copy.wait_recv()

        def sent(*which):
            for copy in copies(*which):
                copy.wait_send()

        def add(block, which, slot):
            combine(block, [array[which].at[slot] for array in arrays])

        def spread(zz):
            def across(i):
                yy = jnp.where(i == 0, 1 - y, y)
                compute_other(at(zz, yy, 1 - core))
                begin(0, zz, yy)

            def here(i):
                yy = jnp.where(i == 0, 1 - y, y)
                block = at(zz, yy, core)
                compute(block)
                received(0, zz, yy)
                add(block, 1, 2 * zz + yy)
                pl.when(i == 0)(lambda: begin(1, zz))

            loop(2, across)
            loop(2, here)

        def along(zz):
            block = at(zz, y, core)
            received(1, zz)
            add(block, 2, zz)

            @pl.when(zz > z)
            def _():
                @pl.when(z > 0)
                def _():
                    received(2, zz)
                    add(block, 3, zz)

                begin(2, zz)

            @pl.when(zz < z)
            def _():
                @pl.when(z + 1 < depth)
                def _():
                    received(3, zz)
                    add(block, 4, zz)

                begin(3, zz)

        def step(i):
            pl.when(i < depth)(lambda: spread(farthest(i)))
            pl.when(i > 0)(lambda: along(farthest(i - 1)))

        loop(depth + 1, step)

        @pl.when(z > 0)
        def _():
            received(2, z)
            add(me, 3, z)

        @pl.when(z + 1 < depth)
        def _():
            received(3, z)
            add(me, 4, z)

        def drain():
            def one(zz):
                sent(0, zz, 0)
                sent(0, zz, 1)
                sent(1, zz)
                pl.when(zz > z)(lambda: sent(2, zz))
                pl.when(zz < z)(lambda: sent(3, zz))

            loop(depth, one)

        drains.append(drain)

    def project(buffer, gain_row, weight, load):
        acc[...] = jnp.zeros_like(acc)
        squares[...] = jnp.zeros_like(squares)

        def term(block):
            part = buffer[block, :rows, :].astype(F32)
            gain = first[block, rows : rows + 16, :].astype(F32)[gain_row : gain_row + 1, :]
            squared = part * part
            total = squared[:, :BLK]
            for start in range(BLK, width, BLK):
                total += squared[:, start : start + BLK]
            squares[...] += total
            depth_rows = pl.ds(pl.multiple_of(block * width, width), width)
            acc[...] += jnp.dot(
                (part * gain).astype(BF16), weight[depth_rows, :], preferred_element_type=F32
            )

        arrive = gather(buffer, load.wait, term)

        def last(i):
            block = 2 * i + 1 - core
            arrive(block)
            term(block)

        loop(n // 2, last)
        mean = jnp.sum(squares[...], axis=1, keepdims=True) * (1.0 / features)
        return acc[...] * lax.rsqrt(mean + EPSILON)

    loads[0].wait()
    query = project(first, 0, qw, loads[1])
    for head in range(heads):
        one = query[:, head * head_dim : (head + 1) * head_dim]
        mean = jnp.mean(one * one, axis=1, keepdims=True)
        queries_all[me, head * rows : (head + 1) * rows, :] = (
            one * lax.rsqrt(mean + EPSILON) * q_gain_ref[...].astype(F32)
        ).astype(BF16)

    factor = head_dim**-0.5 * math.log2(math.e)
    first_block = me * (tokens // BLK)
    chunk = min(2 * rows, heads * rows)

    def attend(block):
        group = (block * heads) // group_size
        columns = pl.ds(pl.multiple_of(group * head_dim, head_dim), head_dim)
        for start in range(0, heads * rows, chunk):
            query_rows = queries_all[block, start : start + chunk, :]
            scores = lax.dot_general(
                query_rows, keys[:, columns], (((1,), (1,)), ((), ())), preferred_element_type=F32
            )
            limit = limits[start : start + chunk, :]
            tiles = [
                jnp.where(
                    limit >= first_block + j, scores[:, j * BLK : (j + 1) * BLK] * factor, -jnp.inf
                )
                for j in range(tokens // BLK)
            ]
            top = functools.reduce(jnp.maximum, tiles)
            top = jnp.maximum(jnp.max(top, axis=1, keepdims=True), -1e30)
            tiles = [jnp.exp2(tile - top) for tile in tiles]
            total = jnp.sum(functools.reduce(jnp.add, tiles), axis=1, keepdims=True)
            weights = jnp.concatenate([tile.astype(BF16) for tile in tiles], axis=1)
            summed = jnp.dot(weights, values[:, columns], preferred_element_type=F32)
            sums[block, start : start + chunk, :] = summed.astype(BF16)
            for inner in range(0, chunk, rows):
                head = (start + inner) // rows
                for row, value in ((head, top), (heads + head, total)):
                    spread = jnp.broadcast_to(value[inner : inner + rows, :], (rows, rows))
                    stats[block, row : row + 1, :] = spread.T[:1, :]

    def merge(block, arrived):
        more_sums, more_stats = arrived
        mine, theirs = stats[block], more_stats[...]
        top = jnp.maximum(mine[:heads], theirs[:heads])
        decay, decay_more = jnp.exp2(mine[:heads] - top), jnp.exp2(theirs[:heads] - top)
        stats[block, :heads, :] = top
        stats[block, heads : 2 * heads, :] = (
            mine[heads : 2 * heads] * decay + theirs[heads : 2 * heads] * decay_more
        )
        for head in range(heads):
            span = slice(head * rows, (head + 1) * rows)
            one = jnp.broadcast_to(decay[head : head + 1, :], (rows, rows)).T
            two = jnp.broadcast_to(decay_more[head : head + 1, :], (rows, rows)).T
            sums[block, span, :] = (
                sums[block, span, :].astype(F32) * one[:, :1]
                + more_sums[span, :].astype(F32) * two[:, :1]
            ).astype(BF16)

    def caches_ready():
        loads[2].wait()
        loads[3].wait()

    arrive = gather(queries_all, caches_ready, attend)

    def attend_late(block):
        arrive(block)
        attend(block)

    reduce(
        [
            (sums, sums_core, sums_y, sums_up, sums_down),
            (stats, stats_core, stats_y, stats_up, stats_down),
        ],
        attend_late,
        lambda block: None,
        merge,
    )
    for head in range(heads):
        total = jnp.broadcast_to(stats[me, heads + head : heads + head + 1, :], (rows, rows)).T
        attended[:, head * head_dim : (head + 1) * head_dim] = (
            sums[me, head * rows : (head + 1) * rows, :].astype(F32) / total[:, :1]
        ).astype(BF16)
    loads[4].wait()

    def mix(block):
        columns = pl.ds(pl.multiple_of(block * width, width), width)
        mixed[block] = jnp.dot(
            attended[...], ow[:, columns], preferred_element_type=F32
        ).astype(BF16)

    def total_of(block, arrived):
        mixed[block] = (mixed[block].astype(F32) + arrived[0][...].astype(F32)).astype(BF16)

    reduce([(mixed, mixed_core, mixed_y, mixed_up, mixed_down)], mix, mix, total_of)
    fresh = (first[me, :rows, :].astype(F32) + mixed[me].astype(F32)).astype(BF16)
    hidden_out[...] = fresh
    second[me] = fresh
    next_out[...] = project(second, 1, nw, loads[5]).astype(BF16)
    for drain in drains:
        drain()


def on_device(
    hidden,
    attn_gain,
    q_weight,
    q_gain,
    key_cache,
    value_cache,
    block_limit,
    out_weight,
    next_gain,
    next_weight,
):
    n = lax.axis_size("ctx")
    depth = n // 4
    rows, width = hidden.shape
    head_dim = q_gain.shape[0]
    heads = width // head_dim
    group_size = heads * n // (key_cache.shape[1] // head_dim)
    tall, lines = heads * rows, max(8, 2 * heads)

    def slots(count):
        return [
            pltpu.VMEM((count, tall, head_dim), BF16),
            pltpu.VMEM((count, lines, rows), F32),
            pltpu.VMEM((count, rows, width), BF16),
        ]

    vmem, hbm = pl.BlockSpec(memory_space=pltpu.VMEM), pl.BlockSpec(memory_space=pl.ANY)
    return pl.pallas_call(
        functools.partial(kernel, n, group_size),
        out_shape=[jax.ShapeDtypeStruct((rows, width), BF16)] * 2,
        in_specs=[vmem] * 5 + [hbm] * 5,
        out_specs=[vmem] * 2,
        scratch_shapes=[
            pltpu.VMEM(q_weight.shape, BF16),
            pltpu.VMEM(key_cache.shape, BF16),
            pltpu.VMEM(value_cache.shape, BF16),
            pltpu.VMEM(out_weight.shape, BF16),
            pltpu.VMEM(next_weight.shape, BF16),
            pltpu.VMEM((n, rows + 16, width), BF16),
            pltpu.VMEM((n, tall, head_dim), BF16),
            pltpu.VMEM((n, rows, width), BF16),
            *slots(n),
            *slots(2 * depth),
            *slots(depth),
            *slots(depth),
            *slots(depth),
            pltpu.VMEM((rows, width), F32),
            pltpu.VMEM((rows, BLK), F32),
            pltpu.VMEM((tall, BLK), jnp.int32),
            pltpu.VMEM((rows, width), BF16),
            pltpu.SemaphoreType.DMA((3 * (n + 5 * depth) + 30 * depth,)),
            pltpu.SemaphoreType.DMA((6,)),
        ],
        compiler_params=pltpu.CompilerParams(
            collective_id=0, has_side_effects=True, vmem_limit_bytes=67043328
        ),
    )(
        hidden,
        attn_gain[None],
        next_gain[None],
        q_gain[None],
        block_limit[None],
        q_weight,
        key_cache,
        value_cache,
        out_weight,
        next_weight,
    )


def solution(mesh):
    in_specs = (
        P("groups", "ctx"),
        P("ctx"),
        P(None, "ctx"),
        P(),
        P(("groups", "ctx"), None),
        P(("groups", "ctx"), None),
        P("groups"),
        P("ctx", None),
        P("ctx"),
        P(None, "ctx"),
    )
    out_specs = (P("groups", "ctx"), P("groups", "ctx"))

    def step(*args):
        return tuple(on_device(*args))

    return jax.shard_map(step, mesh=mesh, in_specs=in_specs, out_specs=out_specs, check_vma=False)
```

profile of v0, /device:TPU:0, one launch (start us, length us, event | category | flops | bytes accessed | tf_op | source)
XLA Modules:
  0.0 128.9 jit_solution(16425636754994460016)
XLA Ops:
  0.6 1.3 broadcast_in_dim.12.attn_gain_ref
  1.9 1.3 broadcast_in_dim.13.next_gain_ref
  3.1 122.6 %shard_map.113 = (bf16[128,512]{1,0:T(8,128)(2,1)}, bf16[128,512]{1,0:T(8,128)(2,1)}) custom-call(bf16[128,512]{1,0:T(8,128)(2,1)} %hidden_in.1, bf16[1,512]{1,0:T(2,128)(2,1)} %broadcast_in_dim.12.attn_gain_ref, bf16[1,512]{1,0:T(2,128)(2,1)} %broadcast_in_dim.13.next_gain_ref, bf16[1,128]{1,0:T(2,128)(2,1)} %bitcast.2, s32[1,128]{1,0:T(1,128)} %bitcast.3, ...), custom_call_target="tpu_custom_call" | custom-call | tf_op jit(solution)/shard_map/pallas_call | solution.py:491
  125.7 1.6 %copy.14 = bf16[128,512]{1,0:T(8,128)(2,1)} copy(bf16[128,512]{1,0:T(8,128)(2,1)} %get-tuple-element.4) | data formatting | bytes 262144
  127.3 1.6 %copy.15 = bf16[128,512]{1,0:T(8,128)(2,1)} copy(bf16[128,512]{1,0:T(8,128)(2,1)} %get-tuple-element.5) | data formatting | bytes 262144
where the time goes:
time: 129 us
  Pallas kernels  123 us (95%)
  local copies, waits for them, and re-layouts  5.65 us (4%)
    pallas_call x1, Pallas kernels, on_device(): pl.pallas_call(functools.partial(kernel, n, group_size), out_shape=[jax.S...  123 us
    unnamed x2, local copies, waits for them, and re-layouts  3.14 us

commit v1 on v0

v1 whole, which is shorter than its diff:
```python
import functools
import math

import jax
import jax.numpy as jnp
from jax import lax
from jax.experimental import pallas as pl
from jax.experimental.pallas import tpu as pltpu
from jax.sharding import PartitionSpec as P

BLK = 128
EPSILON = 1e-05
MESH = pl.DeviceIdType.MESH
BF16, F32 = jnp.bfloat16, jnp.float32


def loop(count, body):
    def step(i, carry):
        body(i)
        return carry

    lax.fori_loop(0, count, step, 0)


def kernel(
    n,
    group_size,
    pieces,
    hidden_in,
    attn_gain_ref,
    next_gain_ref,
    q_gain_ref,
    limit_ref,
    qw_hbm,
    key_hbm,
    value_hbm,
    ow_hbm,
    nw_hbm,
    hidden_out,
    next_out,
    qw,
    keys,
    values,
    ow,
    nw,
    first,
    first_squares,
    queries_all,
    second,
    second_squares,
    sums,
    stats,
    mixed,
    sums_core,
    stats_core,
    mixed_core,
    sums_y,
    stats_y,
    mixed_y,
    sums_up,
    stats_up,
    mixed_up,
    sums_down,
    stats_down,
    mixed_down,
    acc,
    squares,
    limits,
    attended,
    sems,
    local_sems,
):
    depth = n // 4
    me = lax.axis_index("ctx")
    core, y, z = lax.rem(me, 2), lax.rem(me // 2, 2), me // 4
    rows, width = hidden_out.shape
    features = n * width
    head_dim = q_gain_ref.shape[1]
    heads = width // head_dim
    tokens = keys.shape[0]

    def at(zz, yy, cc):
        return zz * 4 + yy * 2 + cc

    other_core, other_y = at(z, y, 1 - core), at(z, 1 - y, core)
    above, below = at(z + 1, y, core), at(z - 1, y, core)

    loads = [
        pltpu.make_async_copy(src, dst, local_sems.at[i])
        for i, (src, dst) in enumerate(
            [(qw_hbm, qw), (key_hbm, keys), (value_hbm, values), (ow_hbm, ow), (nw_hbm, nw)]
        )
    ]
    for load in loads:
        load.start()

    barrier = pltpu.get_barrier_semaphore()

    def greet(device):
        pl.semaphore_signal(barrier, inc=1, device_id={"ctx": device}, device_id_type=MESH)

    greet(other_core)
    greet(other_y)
    pl.when(z + 1 < depth)(lambda: greet(above))
    pl.when(z > 0)(lambda: greet(below))

    def lay_row(column):
        return jnp.broadcast_to(column, (rows, rows)).T[:1, :]

    def lay_column(row):
        return jnp.broadcast_to(row, (rows, rows)).T[:, :1]

    def lane_sums(part):
        squared = part * part
        total = squared[:, :BLK]
        for start in range(BLK, width, BLK):
            total += squared[:, start : start + BLK]
        return total

    own = hidden_in[...].astype(F32)
    first[me] = (own * attn_gain_ref[...].astype(F32)).astype(BF16)
    first_squares[me] = lay_row(jnp.sum(lane_sums(own), axis=1, keepdims=True))

    peers = 2 + jnp.where(z + 1 < depth, 1, 0) + jnp.where(z > 0, 1, 0)
    pl.semaphore_wait(barrier, peers)

    before, after = z, depth - 1 - z
    lone, paired = jnp.abs(after - before), jnp.minimum(after, before)

    def farthest(i):
        j = jnp.maximum(i - lone, 0)
        distance = paired - lax.div(j, 2)
        near = z + jnp.where(lax.rem(j, 2) == 0, distance, -distance)
        return jnp.where(i < lone, jnp.where(after > before, depth - 1 - i, i), near)

    def remote(src, dst, send, recv, device):
        return pltpu.make_async_remote_copy(
            src_ref=src,
            dst_ref=dst,
            send_sem=sems.at[send],
            recv_sem=sems.at[recv],
            device_id={"ctx": device},
            device_id_type=MESH,
        )

    used = [0]
    drains = []

    def take(count):
        used[0] += count
        return used[0] - count

    class Gather:
        def __init__(self, buffer, count, extra=None):
            self.buffer, self.count, self.extra = buffer, count, extra
            self.size = buffer.shape[1] // count
            self.recv, self.send = take(n * count), take(5 * depth)
            if extra is not None:
                self.extra_recv, self.extra_send = take(n), take(5 * depth)
            drains.append(self.drain)

        def copy(self, block, p, device, sem):
            view = self.buffer.at[block, pl.ds(pl.multiple_of(p * self.size, self.size), self.size)]
            return remote(view, view, self.send + sem, self.recv + block * self.count + p, device)

        def extra_copy(self, block, device, sem):
            view = self.extra.at[block]
            return remote(view, view, self.extra_send + sem, self.extra_recv + block, device)

        def whole(self, block, device, sem):
            view = self.buffer.at[block]
            return remote(view, view, self.send + sem, self.recv, device)

        def routes(self, zz):
            return (
                (at(zz, y, core), above, zz),
                (at(zz, y, core), below, depth + zz),
                (at(zz, y, core), other_y, 2 * depth + zz),
            )

        def to_core(self, zz, yy):
            return at(zz, yy, core), other_core, 3 * depth + 2 * zz + yy

        def start(self, route, p):
            block, device, sem = route
            if p is None:
                self.extra_copy(block, device, sem).start()
            else:
                self.copy(block, p, device, sem).start()

        def arrive(self, block, p):
            if p is None:
                self.extra_copy(block, other_core, 0).wait_recv()
            else:
                self.copy(block, p, other_core, 0).wait_recv()

        def arrive_all(self, block):
            loop(self.count, lambda p: self.arrive(block, p))
            if self.extra is not None:
                self.arrive(block, None)

        def begin(self, p):
            up, down, side = self.routes(z)
            pl.when(z + 1 < depth)(lambda: self.start(up, p))
            pl.when(z > 0)(lambda: self.start(down, p))
            self.start(side, p)
            self.start(self.to_core(z, y), p)

        def column(self, distance, sign, p):
            zz = z + sign * distance

            @pl.when((zz >= 0) & (zz < depth))
            def _():
                up, down, side = self.routes(zz)
                self.arrive(at(zz, y, core), p)
                if sign < 0:
                    pl.when(z + 1 < depth)(lambda: self.start(up, p))
                else:
                    pl.when(z > 0)(lambda: self.start(down, p))
                self.start(side, p)
                self.start(self.to_core(zz, y), p)

        def beside(self, distance, sign, p):
            zz = z + sign * distance
            fresh = (distance > 0) if sign > 0 else (distance >= 0)

            @pl.when((zz >= 0) & (zz < depth) & fresh)
            def _():
                self.arrive(at(zz, 1 - y, core), p)
                self.start(self.to_core(zz, 1 - y), p)

        def run(self, ready, consume, consume_late=None):
            def pair(distance, yy, cc, use):
                def one(i):
                    zz = z + jnp.where(i == 0, -distance, distance)
                    fresh = (distance > 0) | ((distance == 0) & (i == 0))

                    @pl.when(fresh & (zz >= 0) & (zz < depth))
                    def _():
                        use(at(zz, yy, cc))

                loop(2, one)

            def late(block):
                self.arrive_all(block)
                consume_late(block)

            def relay(step, p):
                self.column(step, -1, p)
                self.column(step, 1, p)
                self.beside(step - 1, -1, p)
                self.beside(step - 1, 1, p)

            def turn(i):
                step = i + 1

                def inner(p):
                    pl.when(step <= depth)(lambda: relay(step, p))
                    pl.when((step == 1) & (p == 0))(ready)
                    for k in range(4):
                        slot = (k * self.count) // 4

                        @pl.when(p == slot)
                        def _():
                            if k == 0:
                                pair(step - 1, y, core, consume)
                            elif k == 1:
                                pair(step - 2, 1 - y, core, consume)
                            elif consume_late is not None and k == 2:
                                pair(step - 2, y, 1 - core, late)
                            elif consume_late is not None:
                                pair(step - 3, 1 - y, 1 - core, late)

                loop(self.count, inner)
                if self.extra is not None:
                    pl.when(step <= depth)(lambda: relay(step, None))

            loop(depth + 2 if consume_late is not None else depth + 1, turn)

        def drain(self):
            kinds = [self.whole]
            if self.extra is not None:
                kinds.append(self.extra_copy)

            def one(zz):
                up, down, side = self.routes(zz)
                for kind in kinds:
                    pl.when((zz <= z) & (z + 1 < depth))(lambda: kind(*up).wait_send())
                    pl.when((zz >= z) & (z > 0))(lambda: kind(*down).wait_send())
                    kind(*side).wait_send()
                    kind(*self.to_core(zz, 0)).wait_send()
                    kind(*self.to_core(zz, 1)).wait_send()

            loop(depth, one)

    def reduce(arrays, count, compute_other, compute, combine, finish):
        starts = [(take(5 * depth), take(5 * depth * count)) for _ in arrays]

        def copies(kind, p, zz, yy=0):
            made = []
            for (send, recv), (view, part, from_core, from_y, from_below, from_above) in zip(starts, arrays):
                if kind == 0:
                    slot, where = 2 * zz + yy, 0
                    block, dst, device = at(zz, yy, 1 - core), from_core, other_core
                elif kind == 1:
                    slot, where = zz, 2 * depth
                    block, dst, device = at(zz, 1 - y, core), from_y, other_y
                elif kind == 2:
                    slot, where = zz, 3 * depth
                    block, dst, device = at(zz, y, core), from_below, above
                else:
                    slot, where = zz, 4 * depth
                    block, dst, device = at(zz, y, core), from_above, below
                if p is None:
                    src, dst, arrival = part.at[block], dst.at[slot], 0
                else:
                    src, dst, arrival = view(part, block, p), view(dst, slot, p), (where + slot) * count + p
                made.append(remote(src, dst, send + where + slot, recv + arrival, device))
            return made

        def begin(*which):
            for copy in copies(*which):
                copy.start()

        def received(*which):
            for copy in copies(*which):
                copy.wait_recv()

        def sent(*which):
            for copy in copies(*which):
                copy.wait_send()

        def add(block, p, which, slot):
            combine(block, p, [array[0](array[which], slot, p) for array in arrays])

        def spread(zz):
            def across(i):
                yy = jnp.where(i == 0, 1 - y, y)
                compute_other(at(zz, yy, 1 - core))
                loop(count, lambda p: begin(0, p, zz, yy))

            def here(i):
                yy = jnp.where(i == 0, 1 - y, y)
                block = at(zz, yy, core)
                compute(block)

                def one(p):
                    received(0, p, zz, yy)
                    add(block, p, 2, 2 * zz + yy)
                    pl.when(i == 0)(lambda: begin(1, p, zz))

                loop(count, one)

            loop(2, across)
            loop(2, here)

        def along(zz):
            block = at(zz, y, core)

            def one(p):
                received(1, p, zz)
                add(block, p, 3, zz)

                @pl.when(zz > z)
                def _():
                    @pl.when(z > 0)
                    def _():
                        received(2, p, zz)
                        add(block, p, 4, zz)

                    begin(2, p, zz)

                @pl.when(zz < z)
                def _():
                    @pl.when(z + 1 < depth)
                    def _():
                        received(3, p, zz)
                        add(block, p, 5, zz)

                    begin(3, p, zz)

            loop(count, one)

        def step(i):
            pl.when(i < depth)(lambda: spread(farthest(i)))
            pl.when(i > 0)(lambda: along(farthest(i - 1)))

        loop(depth + 1, step)

        def last(p):
            @pl.when(z > 0)
            def _():
                received(2, p, z)
                add(me, p, 4, z)

            @pl.when(z + 1 < depth)
            def _():
                received(3, p, z)
                add(me, p, 5, z)

            finish(p)

        loop(count, last)

        def drain():
            def one(zz):
                sent(0, None, zz, 0)
                sent(0, None, zz, 1)
                sent(1, None, zz)
                pl.when(zz > z)(lambda: sent(2, None, zz))
                pl.when(zz < z)(lambda: sent(3, None, zz))

            loop(depth, one)

        drains.append(drain)

    def project(gathered, weight, load):
        acc[...] = jnp.zeros_like(acc)

        def term(block):
            depth_rows = pl.ds(pl.multiple_of(block * width, width), width)
            acc[...] += jnp.dot(
                gathered.buffer[block], weight[depth_rows, :], preferred_element_type=F32
            )

        gathered.run(load.wait, term, term)
        mean = lay_column(jnp.sum(gathered.extra[...], axis=0)) * (1.0 / features)
        return acc[...] * lax.rsqrt(mean + EPSILON)

    gather_first = Gather(first, pieces, first_squares)
    gather_queries = Gather(queries_all, heads)
    gather_second = Gather(second, pieces, second_squares)

    loop(pieces, gather_first.begin)
    gather_first.begin(None)
    limit_rows = lay_column(limit_ref[...])
    for head in range(heads):
        limits[head * rows : (head + 1) * rows, :] = jnp.broadcast_to(limit_rows, (rows, BLK))

    query = project(gather_first, qw, loads[0])
    for head in range(heads):
        one = query[:, head * head_dim : (head + 1) * head_dim]
        mean = jnp.mean(one * one, axis=1, keepdims=True)
        queries_all[me, head * rows : (head + 1) * rows, :] = (
            one * lax.rsqrt(mean + EPSILON) * q_gain_ref[...].astype(F32)
        ).astype(BF16)
        gather_queries.begin(head)

    factor = head_dim**-0.5 * math.log2(math.e)
    first_block = me * (tokens // BLK)
    chunk = min(2 * rows, heads * rows)

    def attend(block):
        group = (block * heads) // group_size
        columns = pl.ds(pl.multiple_of(group * head_dim, head_dim), head_dim)
        for start in range(0, heads * rows, chunk):
            query_rows = queries_all[block, start : start + chunk, :]
            scores = lax.dot_general(
                query_rows, keys[:, columns], (((1,), (1,)), ((), ())), preferred_element_type=F32
            )
            limit = limits[start : start + chunk, :]
            tiles = [
                jnp.where(
                    limit >= first_block + j, scores[:, j * BLK : (j + 1) * BLK] * factor, -jnp.inf
                )
                for j in range(tokens // BLK)
            ]
            top = functools.reduce(jnp.maximum, tiles)
            top = jnp.maximum(jnp.max(top, axis=1, keepdims=True), -1e30)
            tiles = [jnp.exp2(tile - top) for tile in tiles]
            total = jnp.sum(functools.reduce(jnp.add, tiles), axis=1, keepdims=True)
            weights = jnp.concatenate([tile.astype(BF16) for tile in tiles], axis=1)
            summed = jnp.dot(weights, values[:, columns], preferred_element_type=F32)
            sums[block, start : start + chunk, :] = summed.astype(BF16)
            for inner in range(0, chunk, rows):
                head = (start + inner) // rows
                stats[block, head, 0:1, :] = lay_row(top[inner : inner + rows, :])
                stats[block, head, 1:2, :] = lay_row(total[inner : inner + rows, :])

    def span(head):
        return pl.ds(pl.multiple_of(head * rows, rows), rows)

    def merge(block, head, arrived):
        more_sums, more_stats = arrived
        mine, theirs = stats[block, head], more_stats[...]
        top = jnp.maximum(mine[:1], theirs[:1])
        decay, decay_more = jnp.exp2(mine[:1] - top), jnp.exp2(theirs[:1] - top)
        stats[block, head, 0:1, :] = top
        stats[block, head, 1:2, :] = mine[1:2] * decay + theirs[1:2] * decay_more
        sums[block, span(head), :] = (
            sums[block, span(head), :].astype(F32) * lay_column(decay)
            + more_sums[...].astype(F32) * lay_column(decay_more)
        ).astype(BF16)

    def caches_ready():
        loads[1].wait()
        loads[2].wait()

    gather_queries.run(caches_ready, attend)

    def attend_late(block):
        gather_queries.arrive_all(block)
        attend(block)

    def close(head):
        total = lay_column(stats[me, head, 1:2, :])
        attended[:, pl.ds(pl.multiple_of(head * head_dim, head_dim), head_dim)] = (
            sums[me, span(head), :].astype(F32) / total
        ).astype(BF16)

    def head_view(ref, block, p):
        return ref.at[block, span(p)]

    def stat_view(ref, block, p):
        return ref.at[block, p]

    reduce(
        [
            (head_view, sums, sums_core, sums_y, sums_up, sums_down),
            (stat_view, stats, stats_core, stats_y, stats_up, stats_down),
        ],
        heads,
        attend_late,
        lambda block: None,
        merge,
        close,
    )
    loads[3].wait()

    piece = rows // pieces

    def piece_rows(p):
        return pl.ds(pl.multiple_of(p * piece, piece), piece)

    def row_view(ref, block, p):
        return ref.at[block, piece_rows(p)]

    def mix(block):
        columns = pl.ds(pl.multiple_of(block * width, width), width)
        mixed[block] = jnp.dot(
            attended[...], ow[:, columns], preferred_element_type=F32
        ).astype(BF16)

    def total_of(block, p, arrived):
        mixed[block, piece_rows(p), :] = (
            mixed[block, piece_rows(p), :].astype(F32) + arrived[0][...].astype(F32)
        ).astype(BF16)

    def renew(p):
        span_rows = piece_rows(p)
        fresh = (hidden_in[span_rows, :].astype(F32) + mixed[me, span_rows, :].astype(F32)).astype(BF16)
        hidden_out[span_rows, :] = fresh
        fresh = fresh.astype(F32)
        second[me, span_rows, :] = (fresh * next_gain_ref[...].astype(F32)).astype(BF16)
        squares[span_rows, :] = lane_sums(fresh)
        gather_second.begin(p)

    reduce(
        [(row_view, mixed, mixed_core, mixed_y, mixed_up, mixed_down)], pieces, mix, mix, total_of, renew
    )
    second_squares[me] = lay_row(jnp.sum(squares[...], axis=1, keepdims=True))
    gather_second.begin(None)
    next_out[...] = project(gather_second, nw, loads[4]).astype(BF16)
    for drain in drains:
        drain()


def on_device(
    hidden,
    attn_gain,
    q_weight,
    q_gain,
    key_cache,
    value_cache,
    block_limit,
    out_weight,
    next_gain,
    next_weight,
):
    n = lax.axis_size("ctx")
    depth = n // 4
    rows, width = hidden.shape
    head_dim = q_gain.shape[0]
    heads = width // head_dim
    group_size = heads * n // (key_cache.shape[1] // head_dim)
    tall, pieces = heads * rows, 4

    def slots(count):
        return [
            pltpu.VMEM((count, tall, head_dim), BF16),
            pltpu.VMEM((count, heads, 2, rows), F32),
            pltpu.VMEM((count, rows, width), BF16),
        ]

    semaphores = 2 * n * (pieces + 1) + n * heads + 25 * depth + 5 * depth * (2 * heads + pieces + 3)
    vmem, hbm = pl.BlockSpec(memory_space=pltpu.VMEM), pl.BlockSpec(memory_space=pl.ANY)
    return pl.pallas_call(
        functools.partial(kernel, n, group_size, pieces),
        out_shape=[jax.ShapeDtypeStruct((rows, width), BF16)] * 2,
        in_specs=[vmem] * 5 + [hbm] * 5,
        out_specs=[vmem] * 2,
        scratch_shapes=[
            pltpu.VMEM(q_weight.shape, BF16),
            pltpu.VMEM(key_cache.shape, BF16),
            pltpu.VMEM(value_cache.shape, BF16),
            pltpu.VMEM(out_weight.shape, BF16),
            pltpu.VMEM(next_weight.shape, BF16),
            pltpu.VMEM((n, rows, width), BF16),
            pltpu.VMEM((n, 1, rows), F32),
            pltpu.VMEM((n, tall, head_dim), BF16),
            pltpu.VMEM((n, rows, width), BF16),
            pltpu.VMEM((n, 1, rows), F32),
            *slots(n),
            *slots(2 * depth),
            *slots(depth),
            *slots(depth),
            *slots(depth),
            pltpu.VMEM((rows, width), F32),
            pltpu.VMEM((rows, BLK), F32),
            pltpu.VMEM((tall, BLK), jnp.int32),
            pltpu.VMEM((rows, width), BF16),
            pltpu.SemaphoreType.DMA((semaphores,)),
            pltpu.SemaphoreType.DMA((5,)),
        ],
        compiler_params=pltpu.CompilerParams(
            collective_id=0, has_side_effects=True, vmem_limit_bytes=67043328
        ),
    )(
        hidden,
        attn_gain[None],
        next_gain[None],
        q_gain[None],
        block_limit[None],
        q_weight,
        key_cache,
        value_cache,
        out_weight,
        next_weight,
    )


def solution(mesh):
    in_specs = (
        P("groups", "ctx"),
        P("ctx"),
        P(None, "ctx"),
        P(),
        P(("groups", "ctx"), None),
        P(("groups", "ctx"), None),
        P("groups"),
        P("ctx", None),
        P("ctx"),
        P(None, "ctx"),
    )
    out_specs = (P("groups", "ctx"), P("groups", "ctx"))

    def step(*args):
        return tuple(on_device(*args))

    return jax.shard_map(step, mesh=mesh, in_specs=in_specs, out_specs=out_specs, check_vma=False)
```

time: 129 us -> 129 us (level)
  no operation moved by 1% of the time
where the time goes in v1:
time: 129 us
  Pallas kernels  122 us (95%)
  local copies, waits for them, and re-layouts  5.65 us (4%)
    pallas_call x1, Pallas kernels, on_device(): pl.pallas_call(functools.partial(kernel, n, group_size, pieces), out_shap...  122 us
    unnamed x2, local copies, waits for them, and re-layouts  3.14 us

profile of v1, /device:TPU:0, one launch (start us, length us, event | category | flops | bytes accessed | tf_op | source)
XLA Modules:
  0.0 128.7 jit_solution(15175849857208176441)
XLA Ops:
  0.6 1.3 broadcast_in_dim.12.attn_gain_ref
  1.9 1.3 broadcast_in_dim.13.next_gain_ref
  3.1 122.4 %shard_map.113 = (bf16[128,512]{1,0:T(8,128)(2,1)}, bf16[128,512]{1,0:T(8,128)(2,1)}) custom-call(bf16[128,512]{1,0:T(8,128)(2,1)} %hidden_in.1, bf16[1,512]{1,0:T(2,128)(2,1)} %broadcast_in_dim.12.attn_gain_ref, bf16[1,512]{1,0:T(2,128)(2,1)} %broadcast_in_dim.13.next_gain_ref, bf16[1,128]{1,0:T(2,128)(2,1)} %bitcast.2, s32[1,128]{1,0:T(1,128)} %bitcast.3, ...), custom_call_target="tpu_custom_call" | custom-call | tf_op jit(solution)/shard_map/pallas_call | solution.py:597
  125.5 1.6 %copy.14 = bf16[128,512]{1,0:T(8,128)(2,1)} copy(bf16[128,512]{1,0:T(8,128)(2,1)} %get-tuple-element.4) | data formatting | bytes 262144
  127.1 1.6 %copy.15 = bf16[128,512]{1,0:T(8,128)(2,1)} copy(bf16[128,512]{1,0:T(8,128)(2,1)} %get-tuple-element.5) | data formatting | bytes 262144

commit v2 on v1

--- a/solution.py
+++ b/solution.py
@@ -57,15 +57,13 @@
     sums_y,
     stats_y,
     mixed_y,
-    sums_up,
-    stats_up,
-    mixed_up,
-    sums_down,
-    stats_down,
-    mixed_down,
+    sums_z,
+    stats_z,
+    mixed_z,
     acc,
     squares,
-    limits,
+    bias,
+    marks,
     attended,
     sems,
     local_sems,
@@ -83,7 +81,12 @@
         return zz * 4 + yy * 2 + cc
 
     other_core, other_y = at(z, y, 1 - core), at(z, 1 - y, core)
-    above, below = at(z + 1, y, core), at(z - 1, y, core)
+
+    def others(action):
+        def one(zz):
+            pl.when(zz != z)(lambda: action(zz))
+
+        loop(depth, one)
 
     loads = [
         pltpu.make_async_copy(src, dst, local_sems.at[i])
@@ -101,8 +104,11 @@
 
     greet(other_core)
     greet(other_y)
-    pl.when(z + 1 < depth)(lambda: greet(above))
-    pl.when(z > 0)(lambda: greet(below))
+    others(lambda zz: greet(at(zz, y, core)))
+
+    def wide(gain):
+        lines = gain[...].astype(F32)
+        return jnp.concatenate([lines[i : i + 1, :] for i in range(lines.shape[0])], axis=1)
 
     def lay_row(column):
         return jnp.broadcast_to(column, (rows, rows)).T[:1, :]
@@ -118,11 +124,10 @@
         return total
 
     own = hidden_in[...].astype(F32)
-    first[me] = (own * attn_gain_ref[...].astype(F32)).astype(BF16)
+    first[me] = (own * wide(attn_gain_ref)).astype(BF16)
     first_squares[me] = lay_row(jnp.sum(lane_sums(own), axis=1, keepdims=True))
 
-    peers = 2 + jnp.where(z + 1 < depth, 1, 0) + jnp.where(z > 0, 1, 0)
-    pl.semaphore_wait(barrier, peers)
+    pl.semaphore_wait(barrier, depth + 1)
 
     before, after = z, depth - 1 - z
     lone, paired = jnp.abs(after - before), jnp.minimum(after, before)
@@ -154,9 +159,9 @@
         def __init__(self, buffer, count, extra=None):
             self.buffer, self.count, self.extra = buffer, count, extra
             self.size = buffer.shape[1] // count
-            self.recv, self.send = take(n * count), take(5 * depth)
+            self.recv, self.send = take(n * count), take(4 * depth)
             if extra is not None:
-                self.extra_recv, self.extra_send = take(n), take(5 * depth)
+                self.extra_recv, self.extra_send = take(n), take(4 * depth)
             drains.append(self.drain)
 
         def copy(self, block, p, device, sem):
@@ -171,15 +176,14 @@
             view = self.buffer.at[block]
             return remote(view, view, self.send + sem, self.recv, device)
 
-        def routes(self, zz):
-            return (
-                (at(zz, y, core), above, zz),
-                (at(zz, y, core), below, depth + zz),
-                (at(zz, y, core), other_y, 2 * depth + zz),
-            )
+        def to_z(self, zz):
+            return me, at(zz, y, core), zz
+
+        def to_y(self, zz):
+            return at(zz, y, core), other_y, depth + zz
 
         def to_core(self, zz, yy):
-            return at(zz, yy, core), other_core, 3 * depth + 2 * zz + yy
+            return at(zz, yy, core), other_core, 2 * depth + 2 * zz + yy
 
         def start(self, route, p):
             block, device, sem = route
@@ -200,10 +204,8 @@
                 self.arrive(block, None)
 
         def begin(self, p):
-            up, down, side = self.routes(z)
-            pl.when(z + 1 < depth)(lambda: self.start(up, p))
-            pl.when(z > 0)(lambda: self.start(down, p))
-            self.start(side, p)
+            self.start(self.to_y(z), p)
+            others(lambda zz: self.start(self.to_z(zz), p))
             self.start(self.to_core(z, y), p)
 
         def column(self, distance, sign, p):
@@ -211,13 +213,8 @@
 
             @pl.when((zz >= 0) & (zz < depth))
             def _():
-                up, down, side = self.routes(zz)
                 self.arrive(at(zz, y, core), p)
-                if sign < 0:
-                    pl.when(z + 1 < depth)(lambda: self.start(up, p))
-                else:
-                    pl.when(z > 0)(lambda: self.start(down, p))
-                self.start(side, p)
+                self.start(self.to_y(zz), p)
                 self.start(self.to_core(zz, y), p)
 
         def beside(self, distance, sign, p):
@@ -283,39 +280,34 @@
                 kinds.append(self.extra_copy)
 
             def one(zz):
-                up, down, side = self.routes(zz)
                 for kind in kinds:
-                    pl.when((zz <= z) & (z + 1 < depth))(lambda: kind(*up).wait_send())
-                    pl.when((zz >= z) & (z > 0))(lambda: kind(*down).wait_send())
-                    kind(*side).wait_send()
+                    pl.when(zz != z)(lambda: kind(*self.to_z(zz)).wait_send())
+                    kind(*self.to_y(zz)).wait_send()
                     kind(*self.to_core(zz, 0)).wait_send()
                     kind(*self.to_core(zz, 1)).wait_send()
 
             loop(depth, one)
 
     def reduce(arrays, count, compute_other, compute, combine, finish):
-        starts = [(take(5 * depth), take(5 * depth * count)) for _ in arrays]
+        starts = [(take(4 * depth), take(4 * depth * count)) for _ in arrays]
 
         def copies(kind, p, zz, yy=0):
             made = []
-            for (send, recv), (view, part, from_core, from_y, from_below, from_above) in zip(starts, arrays):
+            for (send, recv), (view, part, from_core, from_y, from_z) in zip(starts, arrays):
+                sender = slot = zz
                 if kind == 0:
-                    slot, where = 2 * zz + yy, 0
-                    block, dst, device = at(zz, yy, 1 - core), from_core, other_core
+                    sender = slot = 2 * zz + yy
+                    where, block, dst, device = 0, at(zz, yy, 1 - core), from_core, other_core
                 elif kind == 1:
-                    slot, where = zz, 2 * depth
-                    block, dst, device = at(zz, 1 - y, core), from_y, other_y
-                elif kind == 2:
-                    slot, where = zz, 3 * depth
-                    block, dst, device = at(zz, y, core), from_below, above
+                    where, block, dst, device = 2 * depth, at(zz, 1 - y, core), from_y, other_y
                 else:
-                    slot, where = zz, 4 * depth
-                    block, dst, device = at(zz, y, core), from_above, below
+                    where, block, dst, device = 3 * depth, at(zz, y, core), from_z, at(zz, y, core)
+                    slot = z if kind == 2 else zz
                 if p is None:
                     src, dst, arrival = part.at[block], dst.at[slot], 0
                 else:
                     src, dst, arrival = view(part, block, p), view(dst, slot, p), (where + slot) * count + p
-                made.append(remote(src, dst, send + where + slot, recv + arrival, device))
+                made.append(remote(src, dst, send + where + sender, recv + arrival, device))
             return made
 
         def begin(*which):
@@ -360,24 +352,7 @@
             def one(p):
                 received(1, p, zz)
                 add(block, p, 3, zz)
-
-                @pl.when(zz > z)
-                def _():
-                    @pl.when(z > 0)
-                    def _():
-                        received(2, p, zz)
-                        add(block, p, 4, zz)
-
-                    begin(2, p, zz)
-
-                @pl.when(zz < z)
-                def _():
-                    @pl.when(z + 1 < depth)
-                    def _():
-                        received(3, p, zz)
-                        add(block, p, 5, zz)
-
-                    begin(3, p, zz)
+                pl.when(zz != z)(lambda: begin(2, p, zz))
 
             loop(count, one)
 
@@ -388,16 +363,11 @@
         loop(depth + 1, step)
 
         def last(p):
-            @pl.when(z > 0)
-            def _():
-                received(2, p, z)
-                add(me, p, 4, z)
-
-            @pl.when(z + 1 < depth)
-            def _():
-                received(3, p, z)
-                add(me, p, 5, z)
-
+            def one(zz):
+                received(3, p, zz)
+                add(me, p, 4, zz)
+
+            others(one)
             finish(p)
 
         loop(count, last)
@@ -407,8 +377,7 @@
                 sent(0, None, zz, 0)
                 sent(0, None, zz, 1)
                 sent(1, None, zz)
-                pl.when(zz > z)(lambda: sent(2, None, zz))
-                pl.when(zz < z)(lambda: sent(3, None, zz))
+                pl.when(zz != z)(lambda: sent(2, None, zz))
 
             loop(depth, one)
 
@@ -433,40 +402,38 @@
 
     loop(pieces, gather_first.begin)
     gather_first.begin(None)
+    factor = head_dim**-0.5 * math.log2(math.e)
+    first_block = me * (tokens // BLK)
+    chunk = min(2 * rows, heads * rows)
+    lanes = lax.broadcasted_iota(jnp.int32, (rows, BLK), 1)
     limit_rows = lay_column(limit_ref[...])
-    for head in range(heads):
-        limits[head * rows : (head + 1) * rows, :] = jnp.broadcast_to(limit_rows, (rows, BLK))
+    for start in range(0, chunk, rows):
+        bias[start : start + rows, :] = jnp.where(limit_rows >= first_block + lanes, 0.0, -1e30).astype(BF16)
+    lanes = lax.broadcasted_iota(jnp.int32, (BLK, BLK), 1)
+    for j in range(tokens // BLK):
+        marks[j * BLK : (j + 1) * BLK, :] = jnp.where(lanes == j, 1.0, 0.0).astype(BF16)
 
     query = project(gather_first, qw, loads[0])
     for head in range(heads):
         one = query[:, head * head_dim : (head + 1) * head_dim]
         mean = jnp.mean(one * one, axis=1, keepdims=True)
         queries_all[me, head * rows : (head + 1) * rows, :] = (
-            one * lax.rsqrt(mean + EPSILON) * q_gain_ref[...].astype(F32)
+            one * lax.rsqrt(mean + EPSILON) * (q_gain_ref[...].astype(F32) * factor)
         ).astype(BF16)
         gather_queries.begin(head)
-
-    factor = head_dim**-0.5 * math.log2(math.e)
-    first_block = me * (tokens // BLK)
-    chunk = min(2 * rows, heads * rows)
 
     def attend(block):
         group = (block * heads) // group_size
         columns = pl.ds(pl.multiple_of(group * head_dim, head_dim), head_dim)
         for start in range(0, heads * rows, chunk):
-            query_rows = queries_all[block, start : start + chunk, :]
+            query_rows = jnp.concatenate([queries_all[block, start : start + chunk, :], bias[...]], axis=1)
+            marked = jnp.concatenate([keys[:, columns], marks[...]], axis=1)
             scores = lax.dot_general(
-                query_rows, keys[:, columns], (((1,), (1,)), ((), ())), preferred_element_type=F32
+                query_rows, marked, (((1,), (1,)), ((), ())), preferred_element_type=F32
             )
-            limit = limits[start : start + chunk, :]
-            tiles = [
-                jnp.where(
-                    limit >= first_block + j, scores[:, j * BLK : (j + 1) * BLK] * factor, -jnp.inf
-                )
-                for j in range(tokens // BLK)
-            ]
+            tiles = [scores[:, j * BLK : (j + 1) * BLK] for j in range(tokens // BLK)]
             top = functools.reduce(jnp.maximum, tiles)
-            top = jnp.maximum(jnp.max(top, axis=1, keepdims=True), -1e30)
+            top = jnp.max(top, axis=1, keepdims=True)
             tiles = [jnp.exp2(tile - top) for tile in tiles]
             total = jnp.sum(functools.reduce(jnp.add, tiles), axis=1, keepdims=True)
             weights = jnp.concatenate([tile.astype(BF16) for tile in tiles], axis=1)
@@ -516,8 +483,8 @@
 
     reduce(
         [
-            (head_view, sums, sums_core, sums_y, sums_up, sums_down),
-            (stat_view, stats, stats_core, stats_y, stats_up, stats_down),
+            (head_view, sums, sums_core, sums_y, sums_z),
+            (stat_view, stats, stats_core, stats_y, stats_z),
         ],
         heads,
         attend_late,
@@ -551,12 +518,12 @@
         fresh = (hidden_in[span_rows, :].astype(F32) + mixed[me, span_rows, :].astype(F32)).astype(BF16)
         hidden_out[span_rows, :] = fresh
         fresh = fresh.astype(F32)
-        second[me, span_rows, :] = (fresh * next_gain_ref[...].astype(F32)).astype(BF16)
+        second[me, span_rows, :] = (fresh * wide(next_gain_ref)).astype(BF16)
         squares[span_rows, :] = lane_sums(fresh)
         gather_second.begin(p)
 
     reduce(
-        [(row_view, mixed, mixed_core, mixed_y, mixed_up, mixed_down)], pieces, mix, mix, total_of, renew
+        [(row_view, mixed, mixed_core, mixed_y, mixed_z)], pieces, mix, mix, total_of, renew
     )
     second_squares[me] = lay_row(jnp.sum(squares[...], axis=1, keepdims=True))
     gather_second.begin(None)
@@ -592,9 +559,9 @@
             pltpu.VMEM((count, rows, width), BF16),
         ]
 
-    semaphores = 2 * n * (pieces + 1) + n * heads + 25 * depth + 5 * depth * (2 * heads + pieces + 3)
+    semaphores = 2 * n * (pieces + 1) + n * heads + 20 * depth + 4 * depth * (2 * heads + pieces + 3)
     vmem, hbm = pl.BlockSpec(memory_space=pltpu.VMEM), pl.BlockSpec(memory_space=pl.ANY)
-    return pl.pallas_call(
+    outs = pl.pallas_call(
         functools.partial(kernel, n, group_size, pieces),
         out_shape=[jax.ShapeDtypeStruct((rows, width), BF16)] * 2,
         in_specs=[vmem] * 5 + [hbm] * 5,
@@ -614,10 +581,10 @@
             *slots(2 * depth),
             *slots(depth),
             *slots(depth),
-            *slots(depth),
             pltpu.VMEM((rows, width), F32),
             pltpu.VMEM((rows, BLK), F32),
-            pltpu.VMEM((tall, BLK), jnp.int32),
+            pltpu.VMEM((min(2 * rows, tall), BLK), BF16),
+            pltpu.VMEM((key_cache.shape[0], BLK), BF16),
             pltpu.VMEM((rows, width), BF16),
             pltpu.SemaphoreType.DMA((semaphores,)),
             pltpu.SemaphoreType.DMA((5,)),
@@ -627,8 +594,8 @@
         ),
     )(
         hidden,
-        attn_gain[None],
-        next_gain[None],
+        attn_gain.reshape(-1, BLK),
+        next_gain.reshape(-1, BLK),
         q_gain[None],
         block_limit[None],
         q_weight,
@@ -637,6 +604,17 @@
         out_weight,
         next_weight,
     )
+    return pl.pallas_call(
+        hand_over,
+        out_shape=[jax.ShapeDtypeStruct((rows, width), BF16)] * 2,
+        in_specs=[vmem] * 2,
+        out_specs=[vmem] * 2,
+    )(*outs)
+
+
+def hand_over(hidden_in, next_in, hidden_out, next_out):
+    hidden_out[...] = hidden_in[...]
+    next_out[...] = next_in[...]
 
 
 def solution(mesh):

time: 129 us -> 124 us (0.961)
  local copies, waits for them, and re-layouts: 5.65 us -> 0 us
    unnamed x2 -> x0, local copies, waits for them, and re-layouts: 3.14 us -> none
    broadcast_in_dim x2 -> x0, local copies, waits for them, and re-layouts: 2.52 us -> none  [the longest x1 1.26 us: on_device(): attn_gain[None]]
    pallas_call x1, Pallas kernels: 122 us -> 120 us  [on_device(): pl.pallas_call(functools.partial(kernel, n, group_size, pieces), out_shap...]
    pallas_call x0 -> x1, Pallas kernels: none -> 1.68 us  [on_device(): pl.pallas_call(hand_over, out_shape=[jax.ShapeDtypeStruct((rows, width),...]
where the time goes in v2:
time: 124 us; the launch traced here: 123 us
  Pallas kernels  122 us (98%)
    pallas_call x1, Pallas kernels, on_device(): pl.pallas_call(functools.partial(kernel, n, group_size, pieces), out_shap...  120 us

profile of v2, /device:TPU:0, one launch (start us, length us, event | category | flops | bytes accessed | tf_op | source)
XLA Modules:
  0.0 122.7 jit_solution(14285087058387047396)
XLA Ops:
  0.6 120.4 %shard_map.113 = (bf16[128,512]{1,0:T(8,128)(2,1)}, bf16[128,512]{1,0:T(8,128)(2,1)}) custom-call(bf16[128,512]{1,0:T(8,128)(2,1)} %hidden_in.1, bf16[4,128]{1,0:T(4,128)(2,1)} %bitcast.4, bf16[4,128]{1,0:T(4,128)(2,1)} %bitcast.5, bf16[1,128]{1,0:T(2,128)(2,1)} %bitcast.6, s32[1,128]{1,0:T(1,128)} %bitcast.7, bf16[8192,512]{1,0:T(8,128)(2,1)} %qw_hbm.1, ...), custom_call_target="tpu_custom_call" | custom-call | tf_op jit(solution)/shard_map/pallas_call | solution.py:564
  121.0 1.7 %shard_map.114 = (bf16[128,512]{1,0:T(8,128)(2,1)}, bf16[128,512]{1,0:T(8,128)(2,1)}) custom-call(bf16[128,512]{1,0:T(8,128)(2,1)} %get-tuple-element.4.hidden_in, bf16[128,512]{1,0:T(8,128)(2,1)} %get-tuple-element.5.next_in), custom_call_target="tpu_custom_call" | custom-call | tf_op jit(solution)/shard_map/pallas_call | solution.py:607

commit v3 on v2

--- a/solution.py
+++ b/solution.py
@@ -226,7 +226,7 @@
                 self.arrive(at(zz, 1 - y, core), p)
                 self.start(self.to_core(zz, 1 - y), p)
 
-        def run(self, ready, consume, consume_late=None):
+        def run(self, ready, consume, consume_late, reach):
             def pair(distance, yy, cc, use):
                 def one(i):
                     zz = z + jnp.where(i == 0, -distance, distance)
@@ -263,16 +263,16 @@
                                 pair(step - 1, y, core, consume)
                             elif k == 1:
                                 pair(step - 2, 1 - y, core, consume)
-                            elif consume_late is not None and k == 2:
-                                pair(step - 2, y, 1 - core, late)
-                            elif consume_late is not None:
-                                pair(step - 3, 1 - y, 1 - core, late)
+                            elif k == 2:
+                                pl.when(step - 2 < reach)(lambda: pair(step - 2, y, 1 - core, late))
+                            else:
+                                pl.when(step - 3 < reach)(lambda: pair(step - 3, 1 - y, 1 - core, late))
 
                 loop(self.count, inner)
                 if self.extra is not None:
                     pl.when(step <= depth)(lambda: relay(step, None))
 
-            loop(depth + 2 if consume_late is not None else depth + 1, turn)
+            loop(max(depth + 1, reach + 2), turn)
 
         def drain(self):
             kinds = [self.whole]
@@ -289,7 +289,7 @@
             loop(depth, one)
 
     def reduce(arrays, count, compute_other, compute, combine, finish):
-        starts = [(take(4 * depth), take(4 * depth * count)) for _ in arrays]
+        starts = [(take(4 * depth), take(2 * depth + 2 * depth * count)) for _ in arrays]
 
         def copies(kind, p, zz, yy=0):
             made = []
@@ -304,9 +304,10 @@
                     where, block, dst, device = 3 * depth, at(zz, y, core), from_z, at(zz, y, core)
                     slot = z if kind == 2 else zz
                 if p is None:
-                    src, dst, arrival = part.at[block], dst.at[slot], 0
+                    src, dst, arrival = part.at[block], dst.at[slot], slot if kind == 0 else 0
                 else:
-                    src, dst, arrival = view(part, block, p), view(dst, slot, p), (where + slot) * count + p
+                    src, dst = view(part, block, p), view(dst, slot, p)
+                    arrival = 2 * depth + (where - 2 * depth + slot) * count + p
                 made.append(remote(src, dst, send + where + sender, recv + arrival, device))
             return made
 
@@ -322,26 +323,23 @@
             for copy in copies(*which):
                 copy.wait_send()
 
-        def add(block, p, which, slot):
-            combine(block, p, [array[0](array[which], slot, p) for array in arrays])
+        def add(block, p, which, *slots):
+            combine(block, p, [[array[0](array[which], slot, p) for array in arrays] for slot in slots])
 
         def spread(zz):
             def across(i):
                 yy = jnp.where(i == 0, 1 - y, y)
                 compute_other(at(zz, yy, 1 - core))
-                loop(count, lambda p: begin(0, p, zz, yy))
+                begin(0, None, zz, yy)
 
             def here(i):
                 yy = jnp.where(i == 0, 1 - y, y)
                 block = at(zz, yy, core)
                 compute(block)
 
-                def one(p):
-                    received(0, p, zz, yy)
-                    add(block, p, 2, 2 * zz + yy)
-                    pl.when(i == 0)(lambda: begin(1, p, zz))
-
-                loop(count, one)
+                received(0, None, zz, yy)
+                combine(block, None, [[array[2].at[2 * zz + yy] for array in arrays]])
+                pl.when(i == 0)(lambda: loop(count, lambda p: begin(1, p, zz)))
 
             loop(2, across)
             loop(2, here)
@@ -363,11 +361,8 @@
         loop(depth + 1, step)
 
         def last(p):
-            def one(zz):
-                received(3, p, zz)
-                add(me, p, 4, zz)
-
-            others(one)
+            others(lambda zz: received(3, p, zz))
+            add(me, p, 4, *[lax.rem(z + k, depth) for k in range(1, depth)])
             finish(p)
 
         loop(count, last)
@@ -392,7 +387,7 @@
                 gathered.buffer[block], weight[depth_rows, :], preferred_element_type=F32
             )
 
-        gathered.run(load.wait, term, term)
+        gathered.run(load.wait, term, term, depth)
         mean = lay_column(jnp.sum(gathered.extra[...], axis=0)) * (1.0 / features)
         return acc[...] * lax.rsqrt(mean + EPSILON)
 
@@ -445,29 +440,35 @@
                 stats[block, head, 1:2, :] = lay_row(total[inner : inner + rows, :])
 
     def span(head):
-        return pl.ds(pl.multiple_of(head * rows, rows), rows)
+        start = head * rows
+        return pl.ds(start if isinstance(head, int) else pl.multiple_of(start, rows), rows)
 
     def merge(block, head, arrived):
-        more_sums, more_stats = arrived
-        mine, theirs = stats[block, head], more_stats[...]
-        top = jnp.maximum(mine[:1], theirs[:1])
-        decay, decay_more = jnp.exp2(mine[:1] - top), jnp.exp2(theirs[:1] - top)
+        if head is None:
+            for one in range(heads):
+                merge(block, one, [[span_sums.at[span(one)], span_stats.at[one]] for span_sums, span_stats in arrived])
+            return
+        marks_all = [stats[block, head]] + [pair[1][...] for pair in arrived]
+        sums_all = [sums[block, span(head), :]] + [pair[0][...] for pair in arrived]
+        top = functools.reduce(jnp.maximum, [mark[:1] for mark in marks_all])
+        decays = [jnp.exp2(mark[:1] - top) for mark in marks_all]
         stats[block, head, 0:1, :] = top
-        stats[block, head, 1:2, :] = mine[1:2] * decay + theirs[1:2] * decay_more
-        sums[block, span(head), :] = (
-            sums[block, span(head), :].astype(F32) * lay_column(decay)
-            + more_sums[...].astype(F32) * lay_column(decay_more)
+        stats[block, head, 1:2, :] = sum(mark[1:2] * decay for mark, decay in zip(marks_all, decays))
+        sums[block, span(head), :] = sum(
+            part.astype(F32) * lay_column(decay) for part, decay in zip(sums_all, decays)
         ).astype(BF16)
 
     def caches_ready():
         loads[1].wait()
         loads[2].wait()
 
-    gather_queries.run(caches_ready, attend)
+    gather_queries.run(caches_ready, attend, attend, 1)
 
     def attend_late(block):
-        gather_queries.arrive_all(block)
-        attend(block)
+        @pl.when(block // 4 != z)
+        def _():
+            gather_queries.arrive_all(block)
+            attend(block)
 
     def close(head):
         total = lay_column(stats[me, head, 1:2, :])
@@ -509,8 +510,9 @@
         ).astype(BF16)
 
     def total_of(block, p, arrived):
-        mixed[block, piece_rows(p), :] = (
-            mixed[block, piece_rows(p), :].astype(F32) + arrived[0][...].astype(F32)
+        span_rows = slice(None) if p is None else piece_rows(p)
+        mixed[block, span_rows, :] = sum(
+            (one[0][...].astype(F32) for one in arrived), mixed[block, span_rows, :].astype(F32)
         ).astype(BF16)
 
     def renew(p):
@@ -559,7 +561,7 @@
             pltpu.VMEM((count, rows, width), BF16),
         ]
 
-    semaphores = 2 * n * (pieces + 1) + n * heads + 20 * depth + 4 * depth * (2 * heads + pieces + 3)
+    semaphores = 2 * n * (pieces + 1) + n * heads + 20 * depth + 2 * depth * (2 * heads + pieces + 9)
     vmem, hbm = pl.BlockSpec(memory_space=pltpu.VMEM), pl.BlockSpec(memory_space=pl.ANY)
     outs = pl.pallas_call(
         functools.partial(kernel, n, group_size, pieces),

time: 124 us -> 122 us (0.984)
    pallas_call x1, Pallas kernels: 120 us -> 119 us  [on_device(): pl.pallas_call(functools.partial(kernel, n, group_size, pieces), out_shap...]
where the time goes in v3:
time: 122 us; the launch traced here: 121 us
  Pallas kernels  121 us (99%)
    pallas_call x1, Pallas kernels, on_device(): pl.pallas_call(functools.partial(kernel, n, group_size, pieces), out_shap...  119 us

profile of v3, /device:TPU:0, one launch (start us, length us, event | category | flops | bytes accessed | tf_op | source)
XLA Modules:
  0.0 121.3 jit_solution(835938247394655230)
XLA Ops:
  0.6 119.0 %shard_map.113 = (bf16[128,512]{1,0:T(8,128)(2,1)}, bf16[128,512]{1,0:T(8,128)(2,1)}) custom-call(bf16[128,512]{1,0:T(8,128)(2,1)} %hidden_in.1, bf16[4,128]{1,0:T(4,128)(2,1)} %bitcast.4, bf16[4,128]{1,0:T(4,128)(2,1)} %bitcast.5, bf16[1,128]{1,0:T(2,128)(2,1)} %bitcast.6, s32[1,128]{1,0:T(1,128)} %bitcast.7, bf16[8192,512]{1,0:T(8,128)(2,1)} %qw_hbm.1, ...), custom_call_target="tpu_custom_call" | custom-call | tf_op jit(solution)/shard_map/pallas_call | solution.py:566
  119.6 1.7 %shard_map.114 = (bf16[128,512]{1,0:T(8,128)(2,1)}, bf16[128,512]{1,0:T(8,128)(2,1)}) custom-call(bf16[128,512]{1,0:T(8,128)(2,1)} %get-tuple-element.4.hidden_in, bf16[128,512]{1,0:T(8,128)(2,1)} %get-tuple-element.5.next_in), custom_call_target="tpu_custom_call" | custom-call | tf_op jit(solution)/shard_map/pallas_call | solution.py:609

commit v4 on v3

--- a/solution.py
+++ b/solution.py
@@ -106,6 +106,12 @@
     greet(other_y)
     others(lambda zz: greet(at(zz, y, core)))
 
+    def near(action):
+        def one(zz):
+            pl.when((zz != z) & (jnp.abs(zz - z) <= 2))(lambda: action(zz))
+
+        loop(depth, one)
+
     def wide(gain):
         lines = gain[...].astype(F32)
         return jnp.concatenate([lines[i : i + 1, :] for i in range(lines.shape[0])], axis=1)
@@ -125,7 +131,6 @@
 
     own = hidden_in[...].astype(F32)
     first[me] = (own * wide(attn_gain_ref)).astype(BF16)
-    first_squares[me] = lay_row(jnp.sum(lane_sums(own), axis=1, keepdims=True))
 
     pl.semaphore_wait(barrier, depth + 1)
 
@@ -159,9 +164,9 @@
         def __init__(self, buffer, count, extra=None):
             self.buffer, self.count, self.extra = buffer, count, extra
             self.size = buffer.shape[1] // count
-            self.recv, self.send = take(n * count), take(4 * depth)
+            self.recv, self.send = take(n * count), take(5 * depth)
             if extra is not None:
-                self.extra_recv, self.extra_send = take(n), take(4 * depth)
+                self.extra_recv, self.extra_send = take(n), take(5 * depth)
             drains.append(self.drain)
 
         def copy(self, block, p, device, sem):
@@ -178,6 +183,13 @@
 
         def to_z(self, zz):
             return me, at(zz, y, core), zz
+
+        def outward(self, zz):
+            beyond = jnp.where(zz < z, z + 1, z - 1)
+            return at(zz, y, core), at(beyond, y, core), 4 * depth + zz
+
+        def passes_on(self, zz):
+            return (jnp.abs(zz - z) >= 2) & jnp.where(zz < z, z + 1 < depth, z > 0)
 
         def to_y(self, zz):
             return at(zz, y, core), other_y, depth + zz
@@ -205,7 +217,7 @@
 
         def begin(self, p):
             self.start(self.to_y(z), p)
-            others(lambda zz: self.start(self.to_z(zz), p))
+            near(lambda zz: self.start(self.to_z(zz), p))
             self.start(self.to_core(z, y), p)
 
         def column(self, distance, sign, p):
@@ -214,6 +226,7 @@
             @pl.when((zz >= 0) & (zz < depth))
             def _():
                 self.arrive(at(zz, y, core), p)
+                pl.when(self.passes_on(zz))(lambda: self.start(self.outward(zz), p))
                 self.start(self.to_y(zz), p)
                 self.start(self.to_core(zz, y), p)
 
@@ -281,7 +294,8 @@
 
             def one(zz):
                 for kind in kinds:
-                    pl.when(zz != z)(lambda: kind(*self.to_z(zz)).wait_send())
+                    pl.when((zz != z) & (jnp.abs(zz - z) <= 2))(lambda: kind(*self.to_z(zz)).wait_send())
+                    pl.when(self.passes_on(zz))(lambda: kind(*self.outward(zz)).wait_send())
                     kind(*self.to_y(zz)).wait_send()
                     kind(*self.to_core(zz, 0)).wait_send()
                     kind(*self.to_core(zz, 1)).wait_send()
@@ -396,6 +410,7 @@
     gather_second = Gather(second, pieces, second_squares)
 
     loop(pieces, gather_first.begin)
+    first_squares[me] = lay_row(jnp.sum(lane_sums(own), axis=1, keepdims=True))
     gather_first.begin(None)
     factor = head_dim**-0.5 * math.log2(math.e)
     first_block = me * (tokens // BLK)
@@ -561,7 +576,7 @@
             pltpu.VMEM((count, rows, width), BF16),
         ]
 
-    semaphores = 2 * n * (pieces + 1) + n * heads + 20 * depth + 2 * depth * (2 * heads + pieces + 9)
+    semaphores = 2 * n * (pieces + 1) + n * heads + 25 * depth + 2 * depth * (2 * heads + pieces + 9)
     vmem, hbm = pl.BlockSpec(memory_space=pltpu.VMEM), pl.BlockSpec(memory_space=pl.ANY)
     outs = pl.pallas_call(
         functools.partial(kernel, n, group_size, pieces),

time: 122 us -> 119 us (0.975)
  Pallas kernels: 121 us -> 118 us
    pallas_call x1, Pallas kernels: 119 us -> 117 us  [on_device(): pl.pallas_call(functools.partial(kernel, n, group_size, pieces), out_shap...]
where the time goes in v4:
time: 119 us
  Pallas kernels  118 us (99%)
    pallas_call x1, Pallas kernels, on_device(): pl.pallas_call(functools.partial(kernel, n, group_size, pieces), out_shap...  117 us

profile of v4, /device:TPU:0, one launch (start us, length us, event | category | flops | bytes accessed | tf_op | source)
XLA Modules:
  0.0 119.1 jit_solution(15645058536724844946)
XLA Ops:
  0.6 116.8 %shard_map.113 = (bf16[128,512]{1,0:T(8,128)(2,1)}, bf16[128,512]{1,0:T(8,128)(2,1)}) custom-call(bf16[128,512]{1,0:T(8,128)(2,1)} %hidden_in.1, bf16[4,128]{1,0:T(4,128)(2,1)} %bitcast.4, bf16[4,128]{1,0:T(4,128)(2,1)} %bitcast.5, bf16[1,128]{1,0:T(2,128)(2,1)} %bitcast.6, s32[1,128]{1,0:T(1,128)} %bitcast.7, bf16[8192,512]{1,0:T(8,128)(2,1)} %qw_hbm.1, ...), custom_call_target="tpu_custom_call" | custom-call | tf_op jit(solution)/shard_map/pallas_call | solution.py:581
  117.4 1.7 %shard_map.114 = (bf16[128,512]{1,0:T(8,128)(2,1)}, bf16[128,512]{1,0:T(8,128)(2,1)}) custom-call(bf16[128,512]{1,0:T(8,128)(2,1)} %get-tuple-element.4.hidden_in, bf16[128,512]{1,0:T(8,128)(2,1)} %get-tuple-element.5.next_in), custom_call_target="tpu_custom_call" | custom-call | tf_op jit(solution)/shard_map/pallas_call | solution.py:624
